TPU v7x, 128 devices: a whole 4x4x4 slice. The times are simulated.
128 devices in a mesh: row: 8 (over z, x_lo), col: 16 (over x_hi, y, core).
Axes of the slice: x: 4 (x_hi: 2, x_lo: 2; x = x_hi * 2 + x_lo), y: 4, z: 4, core: 2. Of those that a mesh axis runs over, the one named last changes fastest.
Arguments:
- t2_pairs: bfloat16 [8, 8, 16, 16, 64, 64], P('row', None, None, None, 'col'), may hold values from -6 to 6
- cycle_ints: bfloat16 [8192, 8192], P('row', 'col'), may hold values from -0.1875 to 0.1875
- eps_occ: float32 [8, 16], replicated, may hold values from -2 to -0.4
- eps_virt: float32 [8, 64], replicated, may hold values from 0.2 to 3
- occ_count: int32 [8], replicated, may hold values from 8 to 16, as said below
- virt_count: int32 [8], replicated, may hold values from 32 to 64, as said below
- window_irrep: int32 [1], replicated, may hold values from 0 to 7
Outputs:
- update: float32 [8192, 8192], P('row', 'col')
Inputs may be any that keep to these rules, and one draw needn't show every extreme that they name: `occ_count`: at least half of the slots; one irrep fills all 16, and another holds exactly the least. `virt_count`: at least half of the slots; one irrep fills all 64, and another holds exactly the least.
All inputs are finite; a program needn't handle non-finite values.
Results may differ from a plain program's by a relative error of at most 0.0003.
Values may be sent and summed in bfloat16 or wider, within the bound.
A program may use at most 128 MiB of HBM per device.

v0:
```python
import jax
import jax.numpy as jnp
from jax import lax
from jax.sharding import PartitionSpec as P

NIRREP = 8
OCC_CAP = 16
VIR_CAP = 64


def ph_vectors(eps_occ, eps_virt, occ_count, virt_count, window_irrep):
    irreps = jnp.arange(NIRREP, dtype=jnp.int32)
    partner = jnp.bitwise_xor(irreps, window_irrep[0])
    onehot = partner[:, None] == irreps[None, :]
    virt_rows = jnp.dot(onehot.astype(jnp.float32), eps_virt, precision=lax.Precision.HIGHEST)
    virt_live = jnp.sum(jnp.where(onehot, virt_count[None, :], 0), axis=1)
    energy = eps_occ[:, None, :] - virt_rows[:, :, None]
    slots_occ = jnp.arange(OCC_CAP, dtype=jnp.int32)
    slots_virt = jnp.arange(VIR_CAP, dtype=jnp.int32)
    live = (slots_occ[None, None, :] < occ_count[:, None, None]) & (
        slots_virt[None, :, None] < virt_live[:, None, None]
    )
    return (energy, live)


def per_device(t2_pairs, cycle_ints, eps_occ, eps_virt, occ_count, virt_count, window_irrep):
    irrep_local = t2_pairs.shape[0]
    virt_local = t2_pairs.shape[4]
    total = NIRREP * VIR_CAP * OCC_CAP
    energy, live = ph_vectors(eps_occ, eps_virt, occ_count, virt_count, window_irrep)
    row_index = lax.axis_index("row")
    col_index = lax.axis_index("col")
    first_irrep = row_index * irrep_local
    first_virt = col_index * virt_local
    zero_index = jnp.int32(0)
    source_live = lax.dynamic_slice(
        live, (first_irrep, first_virt, zero_index), (irrep_local, virt_local, OCC_CAP)
    )
    full_live = live.reshape(-1)
    ordered = jnp.transpose(t2_pairs, (0, 4, 2, 1, 5, 3)).reshape(
        irrep_local, virt_local, OCC_CAP, total
    )
    keep = source_live[:, :, :, None] & full_live[None, None, None, :]
    ordered = jnp.where(keep, ordered, jnp.zeros_like(ordered))
    moved = lax.all_to_all(ordered, "col", split_axis=3, concat_axis=1, tiled=True)
    amp_local = moved.reshape(irrep_local * VIR_CAP * OCC_CAP, moved.shape[3])
    amp_panel = lax.all_gather(amp_local, "row", axis=0, tiled=True)
    ints_panel = lax.all_gather(cycle_ints, "col", axis=1, tiled=True)
    cycle = jnp.dot(ints_panel, amp_panel, preferred_element_type=jnp.float32)
    rows_here = cycle.shape[0]
    cols_here = cycle.shape[1]
    flat_energy = energy.reshape(-1)
    row_start = row_index * rows_here
    col_start = col_index * cols_here
    row_energy = lax.dynamic_slice_in_dim(flat_energy, row_start, rows_here, 0)
    col_energy = lax.dynamic_slice_in_dim(flat_energy, col_start, cols_here, 0)
    row_live = lax.dynamic_slice_in_dim(full_live, row_start, rows_here, 0)
    col_live = lax.dynamic_slice_in_dim(full_live, col_start, cols_here, 0)
    denom = row_energy[:, None] + col_energy[None, :]
    return jnp.where(row_live[:, None] & col_live[None, :], cycle / denom, jnp.float32(0.0))


def solution(mesh):
    placed = (P("row", None, None, None, "col", None), P("row", "col"), P(), P(), P(), P(), P())
    return jax.shard_map(
        per_device, mesh=mesh, in_specs=placed, out_specs=P("row", "col"), check_vma=False
    )
```

profile of v0, /device:TPU:9, one launch (start us, length us, event | category | flops | bytes accessed | tf_op | source)
XLA Modules:
  0.0 405.4 jit_solution(13650713026373814684)
XLA Ops:
  7.2 0.8 select_reduce_fusion
  8.1 0.1 iota_compare_fusion.2
  8.1 0.7 iota_compare_fusion.3
  8.9 0.1 broadcast_and_fusion
  9.0 0.1 and.62
  9.2 7.9 %copy.20 = bf16[1,4,16,8,64,16]{5,4,3,2,1,0:T(8,128)(2,1)} copy(bf16[1,4,16,8,64,16]{4,1,5,2,3,0:T(4,128)(2,1)} %bitcast.23) | data formatting | bytes 2097152 | tf_op jit(solution)/shard_map/transpose | solution.py:40
  17.0 15.1 %reshape.106 = bf16[1,4,16,8192]{3,2,1,0:T(8,128)(2,1)S(1)} reshape(bf16[1,4,16,8,64,16]{5,4,3,2,1,0:T(8,128)(2,1)} %copy.20) | data formatting | bytes 2097152 | tf_op jit(solution)/shard_map/reshape | solution.py:40
  32.2 0.4 and_select_fusion
  32.6 8.3 %copy.21 = bf16[1,4,16,8192]{2,1,0,3:T(4,128)(2,1)} copy(bf16[1,4,16,8192]{3,2,1,0:T(8,128)(2,1)S(1)} %and_select_fusion) | data formatting | bytes 2097152 | tf_op jit(solution)/shard_map/jit(_where)/select_n | solution.py:44
  40.9 10.4 %reshape.108 = bf16[16,2,16384]{2,1,0:T(2,128)(2,1)S(1)} reshape(bf16[8192,1,4,16]{3,2,1,0:T(4,128)(2,1)} %bitcast.19) | data formatting | bytes 2097152
  51.3 22.5 %all_to_all.15 = bf16[16,2,16384]{2,1,0:T(2,128)(2,1)S(1)} all-to-all(bf16[16,2,16384]{2,1,0:T(2,128)(2,1)S(1)} %reshape.108), channel_id=1, replica_groups=mesh['row'=8,'col'=16] {'col'}, dimensions={0} | all-to-all | bytes 2097152 | tf_op jit(solution)/shard_map/all_to_all | solution.py:45
  73.9 7.5 %reshape.109 = bf16[8192,1,4,16]{3,2,1,0:T(4,128)(2,1)} reshape(bf16[16,2,16384]{2,1,0:T(2,128)(2,1)S(1)} %all_to_all.15) | data formatting | bytes 2097152
  81.4 8.6 %copy.25 = bf16[1,4,16,16,512]{4,3,2,1,0:T(8,128)(2,1)S(1)} copy(bf16[1,4,16,16,512]{2,1,4,3,0:T(4,128)(2,1)} %bitcast.20) | data formatting | bytes 2097152 | tf_op jit(solution)/shard_map/all_to_all | solution.py:45
  90.0 1.5 copy.23
  91.6 0.7 all-gather.5.cloned.1.call-update
  92.4 0.1 dynamic_slice.16
  92.4 0.2 fusion.1
  92.6 0.1 broadcast_subtract_fusion
  92.8 0.1 sub.20
  92.9 0.1 dynamic_slice.19
  93.0 167.4 %all-gather.3.cloned.1.call-done = bf16[8192,512]{1,0:T(8,128)(2,1)} async-done(((bf16[1024,512]{1,0:T(8,128)(2,1)}), bf16[8192,512]{1,0:T(8,128)(2,1)}) %all-gather.3.cloned.1.call-update) | async-done | bytes 8388624 | tf_op jit(solution)/shard_map/all_gather | solution.py:47
  260.4 120.7 %all-gather.5.cloned.1.call-done = bf16[1024,8192]{1,0:T(8,128)(2,1)} async-done(((bf16[1024,512]{1,0:T(8,128)(2,1)}), bf16[1024,8192]{1,0:T(8,128)(2,1)}) %all-gather.5.cloned.1.call-update) | async-done | bytes 16777232 | tf_op jit(solution)/shard_map/all_gather | solution.py:48
  381.1 15.7 %fusion = f32[1024,512]{0,1:T(8,128)S(1)} fusion(bf16[8192,512]{1,0:T(8,128)(2,1)} %all-gather.3.cloned.1.call-done, bf16[1024,8192]{1,0:T(8,128)(2,1)} %all-gather.5.cloned.1.call-done, f32[512]{0:T(512)S(1)} %dynamic_slice.19, f32[1024]{0:T(1024)S(1)} %dynamic_slice.18, pred[1024]{0:T(1024)(128)(4,1)S(1)} %dynamic_slice.15, ...), kind=kOutput, calls=%fused_computation.1 | convolution fusion | flops 8592031744 | bytes 27270656 | tf_op jit(solution)/shard_map/dot_general | solution.py:49
  396.8 1.8 copy.24
  (11 shorter events, 0.1 us)
Async XLA Ops:
  6.5 85.9 %copy-start = (f32[8,64]{1,0:T(8,128)S(1)}, f32[8,64]{1,0:T(8,128)}, u32[]{:S(2)}) copy-start(f32[8,64]{1,0:T(8,128)} %param.10) | copy-start | bytes 6148
  6.5 253.8 %all-gather.3.cloned.1.call-start = ((), (), s32[]{:S(2)}) async-start(), calls=%async_computation.1 | async-start | bytes 9437184 | tf_op jit(solution)/shard_map/all_gather | solution.py:47
  81.4 11.2 %copy-start.1 = (f32[8,16]{1,0:T(8,128)S(1)}, f32[8,16]{1,0:T(8,128)}, u32[]{:S(2)}) copy-start(f32[8,16]{1,0:T(8,128)} %param.9) | copy-start | bytes 1540
  91.6 289.5 %all-gather.5.cloned.1.call-start = ((), (), s32[]{:S(2)}) async-start(), calls=%async_computation.2 | async-start | bytes 17825792 | tf_op jit(solution)/shard_map/all_gather | solution.py:48
Sparse Core Ops, SparseCore 0:
  91.7 168.6 all-gather.2
  262.6 118.3 all-gather.4
where the time goes:
time: 409 us; the launch traced here: 405 us
  waiting for transfers between devices  289 us (71%)
  local copies, waits for them, and re-layouts  61.7 us (15%)
  blocking collectives  22.5 us (6%)
  matrix products  15.9 us (4%)
  between operations  14.2 us (3%)
    all_gather x1, waiting for transfers between devices, per_device(): amp_panel = lax.all_gather(amp_local, 'row', axis=0, tiled=True)  167 us
    all_gather x1, waiting for transfers between devices, per_device(): ints_panel = lax.all_gather(cycle_ints, 'col', axis=1, tiled=True)  121 us
    all_to_all x1, blocking collectives, per_device(): lax.all_to_all(ordered, 'col', split_axis=3, concat_axis=1, tiled=True)  22.5 us
    unnamed x6, local copies, waits for them, and re-layouts  18 us
    dot_general x1, matrix products, per_device(): cycle = jnp.dot(ints_panel, amp_panel, preferred_element_type=jnp.float32)  15.7 us
    reshape x1, local copies, waits for them, and re-layouts, per_device(): jnp.transpose(t2_pairs, (0, 4, 2, 1, 5, 3))  15.1 us
    all_to_all x2, local copies, waits for them, and re-layouts, per_device(): lax.all_to_all(ordered, 'col', split_axis=3, concat_axis=1, tiled=True)  10.1 us
    select_n x1, local copies, waits for them, and re-layouts, per_device(): ordered = jnp.where(keep, ordered, jnp.zeros_like(ordered))  8.33 us
  transfers between devices with their start and end apart: 2, of which 2 were waited for; matrix products, arithmetic and copies ran while one was open for 0% of the time, Pallas kernels for 0%

commit v1 on v0

v1 whole, which is shorter than its diff:
```python
import jax
import jax.numpy as jnp
from jax import lax
from jax.experimental import pallas as pl
from jax.experimental.pallas import tpu as pltpu
from jax.sharding import PartitionSpec as P

MESH = pl.DeviceIdType.MESH
NIRREP = 8
OCC = 16
VIR = 64
BLOCK = 512
ROWS = 1024
HALF = 512
N_SENDS = 80


def kernel(x_ref, w_ref, eocc, evirt, nocc, nvirt, window, out_ref,
           wbuf, tbuf, abuf, s32, lhs, inv, w_rs, s_rs, t_rs, a_rs, ss, loc):
    row = lax.axis_index("row")
    col = lax.axis_index("col")
    z, xl = row // 2, row % 2
    xh, y, core = col // 8, (col // 2) % 4, col % 2
    g = window[0]

    def col_of(a, b, k):
        return a * 8 + b * 2 + k

    y_up = (row, col_of(xh, (y + 1) % 4, core))
    y_dn = (row, col_of(xh, (y + 3) % 4, core))
    x_far = (row, col_of(1 - xh, y, core))
    sibling = (row, col_of(xh, y, 1 - core))
    z_up = (((z + 1) % 4) * 2 + xl, col)
    z_dn = (((z + 3) % 4) * 2 + xl, col)
    x_near = (z * 2 + 1 - xl, col)
    a2a = [(dx, dy, dk) for dx in range(2) for dy in range(4) for dk in range(2)
           if (dx, dy, dk) != (0, 0, 0)]

    def peer(d):
        return col_of((xh + d[0]) % 2, (y + d[1]) % 4, (core + d[2]) % 2)

    barrier = pltpu.get_barrier_semaphore()
    for d in a2a:
        pl.semaphore_signal(barrier, inc=1, device_id=(row, peer(d)), device_id_type=MESH)
    for dev in (z_up, z_dn, x_near):
        pl.semaphore_signal(barrier, inc=1, device_id=dev, device_id_type=MESH)

    mine = pltpu.make_async_copy(w_ref, wbuf.at[xh * 4 + y, core], loc)
    mine.start()

    rid = lax.broadcasted_iota(jnp.int32, (64, 128), 0)
    lane = lax.broadcasted_iota(jnp.int32, (64, 128), 1)
    live_src = (rid % OCC < nocc[row]) & (col * 4 + rid // OCC < nvirt[row ^ g])

    def prepare(h2, _):
        for p in range(OCC):
            s32[pl.ds(p, 64, stride=OCC), 0:VIR] = x_ref[h2, p].astype(jnp.float32)
        for pair in range(8):
            lo = s32[pl.ds(pair * 128, 64), :]
            hi = pltpu.roll(s32[pl.ds(pair * 128 + 64, 64), :], 64, 1)
            both = jnp.where(live_src, jnp.where(lane < VIR, lo, hi), 0.0)
            lhs[pl.ds(h2 * 64, 64), pl.ds(pair * 128, 128)] = both.astype(jnp.bfloat16)
        return 0

    lax.fori_loop(0, NIRREP, prepare, 0)
    mine.wait()
    pl.semaphore_wait(barrier, len(a2a) + 3)

    sends = []

    def push(src, dst, rsem, dev):
        cp = pltpu.make_async_remote_copy(
            src_ref=src, dst_ref=dst, send_sem=ss.at[len(sends)], recv_sem=rsem,
            device_id=dev, device_id_type=MESH)
        cp.start()
        sends.append(cp)

    def arrived(ref, rsem):
        pltpu.make_async_remote_copy(
            src_ref=ref, dst_ref=ref, send_sem=ss.at[N_SENDS - 1], recv_sem=rsem,
            device_id=sibling, device_id_type=MESH).wait_recv()

    def wslot(da, db, j, k):
        return wbuf.at[((xh + da) % 2) * 4 + (y + db) % 4, k, pl.ds(j * HALF, HALF)]

    def w_up(da, db, j):
        s = wslot(da, db, j, core)
        push(s, s, w_rs.at[da, (db + 3) % 4, j], y_up)

    def w_dn(da, db, j):
        s = wslot(da, db, j, core)
        push(s, s, w_rs.at[da, (db + 1) % 4, j], y_dn)

    def w_far(da, db, j):
        s = wslot(da, db, j, core)
        push(s, s, w_rs.at[1 - da, db, j], x_far)

    def w_sib(da, db, j):
        s = wslot(da, db, j, core)
        push(s, s, s_rs.at[da, db, j], sibling)

    def w_in(da, db, j):
        arrived(wslot(da, db, j, core), w_rs.at[da, db, j])
        w_sib(da, db, j)

    def tslot(da, db, j):
        return tbuf.at[((z + db) % 4) * 2 + (xl + da) % 2, pl.ds(((xh + j) % 2) * HALF, HALF)]

    def t_up(da, db, j):
        s = tslot(da, db, j)
        push(s, s, t_rs.at[da, (db + 3) % 4, j], z_up)

    def t_dn(da, db, j):
        s = tslot(da, db, j)
        push(s, s, t_rs.at[da, (db + 1) % 4, j], z_dn)

    def t_near(da, db, j):
        s = tslot(da, db, j)
        push(s, s, t_rs.at[1 - da, db, j], x_near)

    def t_in(da, db, j):
        arrived(tslot(da, db, j), t_rs.at[da, db, j])

    w_up(0, 0, 0)
    w_dn(0, 0, 1)
    w_far(0, 0, 0)
    w_far(0, 0, 1)
    w_sib(0, 0, 0)
    w_sib(0, 0, 1)

    src = lax.broadcasted_iota(jnp.int32, (1024, 256), 0)
    dst = lax.broadcasted_iota(jnp.int32, (1024, 256), 1)
    code = (src % VIR) * OCC + src // VIR
    for n in range(4):
        onehot = jnp.where(code == dst + n * 256, 1.0, 0.0).astype(jnp.bfloat16)
        moved = jnp.dot(lhs[...], onehot, preferred_element_type=jnp.float32).astype(jnp.bfloat16)
        for h2 in range(NIRREP):
            abuf[h2 * 2 + n // 2, :, (n % 2) * 256:(n % 2) * 256 + 256] = moved[h2 * 64:h2 * 64 + 64, :]

    place = pl.multiple_of(col * 64, 64)

    def piece(c):
        return tbuf.at[row, pl.ds(pl.multiple_of(c * 64, 64), 64)]

    for i, d in enumerate(a2a):
        push(abuf.at[peer(d)], piece(col), a_rs.at[i], (row, peer(d)))
    tbuf[row, pl.ds(place, 64), :] = abuf[col]

    w_up(0, 0, 1)
    w_dn(0, 0, 0)

    h2 = col // 2
    jj = lax.broadcasted_iota(jnp.int32, (OCC, BLOCK), 1)
    ii = lax.broadcasted_iota(jnp.int32, (OCC, BLOCK), 0)
    c_occ = jnp.zeros((OCC, BLOCK), jnp.float32)
    r_occ = jnp.zeros((OCC, BLOCK), jnp.float32)
    for p in range(OCC):
        c_occ = jnp.where(jj % OCC == p, eocc[h2, p], c_occ)
        r_occ = jnp.where(ii == p, eocc[row, p], r_occ)
    c_vir = jnp.zeros((OCC, BLOCK), jnp.float32)
    for q in range(32):
        c_vir = jnp.where(jj // OCC == q, evirt[h2 ^ g, core * 32 + q], c_vir)
    c_e = c_occ - c_vir
    ok = (jj % OCC < nocc[h2]) & (core * 32 + jj // OCC < nvirt[h2 ^ g]) & (ii < nocc[row])
    n_row = nvirt[row ^ g]

    def factor(q, _):
        e = (r_occ - evirt[row ^ g, q]) + c_e
        inv[pl.ds(pl.multiple_of(q * OCC, OCC), OCC), :] = jnp.where(ok & (q < n_row), 1.0 / e, 0.0)
        return 0

    lax.fori_loop(0, VIR, factor, 0)

    for half in range(2):
        for i, d in enumerate(a2a):
            if d[0] == half:
                c_from = col_of((xh + d[0]) % 2, (y + 4 - d[1]) % 4, (core + d[2]) % 2)
                arrived(piece(c_from), a_rs.at[i])
        t_up(0, 0, half)
        t_dn(0, 0, half)
        t_near(0, 0, half)

    w_in(0, 3, 0)
    w_up(0, 3, 0)
    w_in(0, 1, 1)
    w_dn(0, 1, 1)
    for j in range(2):
        w_in(1, 0, j)
        w_up(1, 0, j)
        w_dn(1, 0, j)
    t_in(0, 3, 0)
    t_up(0, 3, 0)
    t_in(0, 1, 1)
    t_dn(0, 1, 1)
    for j in range(2):
        t_in(1, 0, j)
        t_up(1, 0, j)
        t_dn(1, 0, j)
    w_in(0, 3, 1)
    w_in(0, 1, 0)
    t_in(0, 3, 1)
    t_in(0, 1, 0)
    w_in(0, 2, 0)
    w_in(0, 2, 1)
    for j in range(2):
        t_in(0, 2, j)
        t_near(0, 2, j)
    w_in(1, 3, 0)
    w_up(1, 3, 0)
    w_in(1, 1, 1)
    w_dn(1, 1, 1)
    w_in(1, 3, 1)
    w_in(1, 1, 0)
    for j in range(2):
        t_in(1, 3, j)
        t_in(1, 1, j)
    for j in range(2):
        w_in(1, 2, j)
        t_in(1, 2, j)
    for da in range(2):
        for db in range(4):
            for j in range(2):
                arrived(wslot(da, db, j, 1 - core), s_rs.at[da, db, j])

    out_ref[...] = jnp.zeros_like(out_ref)

    def product(i, _):
        h, m = i // 4, i % 4
        rows = pl.ds(pl.multiple_of(m * 256, 256), 256)
        part = jnp.dot(wbuf[h, 0, rows, :], tbuf[h, 0:512, :], preferred_element_type=jnp.float32)
        part += jnp.dot(wbuf[h, 1, rows, :], tbuf[h, 512:1024, :], preferred_element_type=jnp.float32)
        out_ref[rows, :] += part
        return 0

    lax.fori_loop(0, 32, product, 0)
    out_ref[...] = out_ref[...] * inv[...]
    for cp in sends:
        cp.wait_send()


def per_device(t2_pairs, cycle_ints, eps_occ, eps_virt, occ_count, virt_count, window_irrep):
    amps = t2_pairs.reshape(NIRREP, OCC, OCC * t2_pairs.shape[4], VIR)
    vmem = pl.BlockSpec(memory_space=pltpu.VMEM)
    smem = pl.BlockSpec(memory_space=pltpu.SMEM)
    return pl.pallas_call(
        kernel,
        out_shape=jax.ShapeDtypeStruct((ROWS, BLOCK), jnp.float32),
        in_specs=[vmem, pl.BlockSpec(memory_space=pl.ANY), smem, smem, smem, smem, smem],
        out_specs=vmem,
        scratch_shapes=[
            pltpu.VMEM((NIRREP, 2, ROWS, BLOCK), jnp.bfloat16),
            pltpu.VMEM((NIRREP, ROWS, BLOCK), jnp.bfloat16),
            pltpu.VMEM((16, 64, BLOCK), jnp.bfloat16),
            pltpu.VMEM((1024, 128), jnp.float32),
            pltpu.VMEM((512, 1024), jnp.bfloat16),
            pltpu.VMEM((ROWS, BLOCK), jnp.float32),
            pltpu.SemaphoreType.DMA((2, 4, 2)),
            pltpu.SemaphoreType.DMA((2, 4, 2)),
            pltpu.SemaphoreType.DMA((2, 4, 2)),
            pltpu.SemaphoreType.DMA((15,)),
            pltpu.SemaphoreType.DMA((N_SENDS,)),
            pltpu.SemaphoreType.DMA,
        ],
        compiler_params=pltpu.CompilerParams(
            collective_id=0, has_side_effects=True, vmem_limit_bytes=52 << 20),
    )(amps, cycle_ints, eps_occ, eps_virt, occ_count, virt_count, window_irrep)


def solution(mesh):
    placed = (P("row", None, None, None, "col", None), P("row", "col"), P(), P(), P(), P(), P())
    return jax.shard_map(
        per_device, mesh=mesh, in_specs=placed, out_specs=P("row", "col"), check_vma=False
    )
```

time: 409 us -> 122 us (0.30)
  waiting for transfers between devices: 289 us -> 0 us
  Pallas kernels: 0 us -> 113 us
  local copies, waits for them, and re-layouts: 61.7 us -> 6.98 us
  blocking collectives: 22.5 us -> 0 us
  matrix products: 15.9 us -> 0 us
  between operations: 14.2 us -> 0.67 us
    all_gather x2 -> x0, waiting for transfers between devices: 288 us -> none  [the longest x1 167 us: per_device(): amp_panel = lax.all_gather(amp_local, 'row', axis=0, tiled=True)]
    pallas_call x0 -> x1, Pallas kernels: none -> 113 us  [per_device(): pl.pallas_call(kernel, out_shape=jax.ShapeDtypeStruct((ROWS, BLOCK), jnp....]
    all_to_all x1 -> x0, blocking collectives: 22.5 us -> none  [per_device(): lax.all_to_all(ordered, 'col', split_axis=3, concat_axis=1, tiled=True)]
    dot_general x2 -> x0, matrix products: 15.9 us -> none  [the longest x1 15.7 us: per_device(): cycle = jnp.dot(ints_panel, amp_panel, preferred_element_type=jnp.float32)]
    reshape x1 -> x0, local copies, waits for them, and re-layouts: 15.1 us -> none  [per_device(): jnp.transpose(t2_pairs, (0, 4, 2, 1, 5, 3))]
    unnamed x6 -> x11, local copies, waits for them, and re-layouts: 18 us -> 6.98 us
    select_n x2 -> x0, local copies, waits for them, and re-layouts: 10.1 us -> none  [the longest x1 8.33 us: per_device(): ordered = jnp.where(keep, ordered, jnp.zeros_like(ordered))]
    all_to_all x2 -> x0, local copies, waits for them, and re-layouts: 10.1 us -> none  [per_device(): lax.all_to_all(ordered, 'col', split_axis=3, concat_axis=1, tiled=True)]
  transfers between devices with their start and end apart: 2 -> 0, of which waited for: 2 -> 0; matrix products, arithmetic and copies ran while one was open for 0% -> 0% of each run, Pallas kernels for 0% -> 0%
where the time goes in v1:
time: 122 us; the launch traced here: 121 us
  Pallas kernels  113 us (93%)
  local copies, waits for them, and re-layouts  6.98 us (6%)
    pallas_call x1, Pallas kernels, per_device(): pl.pallas_call(kernel, out_shape=jax.ShapeDtypeStruct((ROWS, BLOCK), jnp....  113 us
    unnamed x11, local copies, waits for them, and re-layouts  6.98 us

profile of v1, /device:TPU:9, one launch (start us, length us, event | category | flops | bytes accessed | tf_op | source)
XLA Modules:
  0.0 121.1 jit_solution(14340355009071036262)
XLA Ops:
  0.7 0.0 copy-start
  0.7 1.2 %copy-done = bf16[1024,512]{1,0:T(8,128)(2,1)S(1)} copy-done((bf16[1024,512]{1,0:T(8,128)(2,1)S(1)}, bf16[1024,512]{1,0:T(8,128)(2,1)}, u32[]{:S(2)}) %copy-start) | copy-done | bytes 1048600
  1.9 0.0 copy-start.1
  1.9 0.7 copy-done.1
  2.6 0.0 copy-start.2
  2.6 0.7 copy-done.2
  3.3 0.0 copy-start.3
  3.3 0.7 copy-done.3
  3.9 0.0 copy-start.4
  3.9 0.7 copy-done.4
  4.6 113.4 %shard_map.73 = f32[1024,512]{1,0:T(8,128)} custom-call(bf16[8,16,64,64]{3,2,1,0:T(8,128)(2,1)} %bitcast.1, bf16[1024,512]{1,0:T(8,128)(2,1)S(1)} %copy-done, f32[8,16]{1,0:T(8,128)S(1)} %copy-done.1, f32[8,64]{1,0:T(8,128)S(1)} %copy-done.2, s32[8]{0:T(128)S(1)} %copy-done.3, s32[8]{0:T(128)S(1)} %copy-done.4, s32[1]{0:T(128)S(6)} %copy.9.window), custom_call_target="tpu_custom_call" | custom-call | tf_op jit(solution)/shard_map/pallas_call | solution.py:245
  118.0 3.1 %copy.10 = f32[1024,512]{1,0:T(8,128)} copy(f32[1024,512]{1,0:T(8,128)} %shard_map.73) | data formatting | bytes 4194304
Async XLA Ops:
  0.7 1.2 %copy-start = (bf16[1024,512]{1,0:T(8,128)(2,1)S(1)}, bf16[1024,512]{1,0:T(8,128)(2,1)}, u32[]{:S(2)}) copy-start(bf16[1024,512]{1,0:T(8,128)(2,1)} %w_ref.1) | copy-start | bytes 3145732
  1.9 0.7 copy-start.1
  2.6 0.7 copy-start.2
  3.3 0.7 copy-start.3
  3.9 0.7 copy-start.4

commit v2 on v1

v2 whole, which is shorter than its diff:
```python
import jax
import jax.numpy as jnp
from jax import lax
from jax.experimental import pallas as pl
from jax.experimental.pallas import tpu as pltpu
from jax.sharding import PartitionSpec as P

MESH = pl.DeviceIdType.MESH
NIRREP = 8
OCC = 16
VIR = 64
BLOCK = 512
ROWS = 1024
PART = 256
TILE = 512
N_SENDS = 110
DEPTH = 2
FIRST = [("w_up", 0, 0, 0), ("w_dn", 0, 0, 2), ("w_far", 0, 0, 0)]
ORDER = [
    ("w_up", 0, 0, 0), ("w_dn", 0, 0, 2), ("w_far", 0, 0, 0), ("w_up", 0, 0, 1), ("w_dn", 0, 0, 3),
    ("w_in", 0, 3, 0), ("w_in", 0, 1, 2), ("w_in", 1, 0, 0), ("t_in", 0, 0, 0), ("t_up", 0, 0, 0),
    ("t_dn", 0, 0, 0), ("t_near", 0, 0, 0), ("t_in", 0, 0, 1), ("t_up", 0, 0, 1),
    ("t_dn", 0, 0, 1), ("t_in", 0, 0, 2), ("t_up", 0, 0, 2), ("t_dn", 0, 0, 2), ("t_in", 0, 3, 0),
    ("t_in", 0, 1, 0), ("w_up", 0, 0, 2), ("w_dn", 0, 0, 0), ("w_far", 0, 0, 2), ("t_in", 0, 0, 3),
    ("t_up", 0, 0, 3), ("t_dn", 0, 0, 3), ("t_in", 0, 3, 1), ("t_in", 0, 1, 1), ("w_up", 0, 0, 3),
    ("w_dn", 0, 0, 1), ("t_near", 0, 0, 1), ("w_in", 0, 3, 1), ("w_in", 0, 1, 3),
    ("t_in", 1, 0, 0), ("t_up", 0, 3, 0), ("t_in", 0, 3, 2), ("t_in", 0, 1, 2), ("t_dn", 0, 1, 2),
    ("w_up", 0, 3, 0), ("w_dn", 0, 1, 2), ("w_far", 0, 0, 1), ("w_in", 0, 3, 2), ("w_in", 0, 1, 0),
    ("w_in", 1, 0, 2), ("t_up", 0, 3, 1), ("t_in", 0, 3, 3), ("t_in", 0, 1, 3), ("t_dn", 0, 1, 3),
    ("w_up", 0, 3, 1), ("w_dn", 0, 1, 3), ("t_near", 0, 0, 2), ("w_in", 0, 3, 3),
    ("w_in", 0, 1, 1), ("t_in", 1, 0, 1), ("prod", 0), ("t_up", 1, 0, 0), ("t_dn", 1, 0, 0),
    ("t_in", 0, 2, 0), ("t_in", 0, 2, 2), ("w_up", 1, 0, 0), ("w_dn", 1, 0, 2), ("w_far", 0, 0, 3),
    ("w_in", 0, 2, 0), ("w_in", 0, 2, 2), ("w_in", 1, 0, 1), ("t_up", 1, 0, 1), ("t_dn", 1, 0, 1),
    ("t_in", 0, 2, 1), ("t_in", 0, 2, 3), ("w_up", 1, 0, 2), ("w_dn", 1, 0, 0),
    ("t_near", 0, 0, 3), ("w_in", 0, 2, 1), ("w_in", 0, 2, 3), ("t_in", 1, 0, 2), ("prod", 1),
    ("t_up", 1, 0, 2), ("t_dn", 1, 0, 2), ("t_in", 1, 3, 0), ("t_in", 1, 1, 0), ("w_up", 1, 0, 1),
    ("t_near", 0, 2, 1), ("w_in", 1, 3, 0), ("w_in", 1, 1, 2), ("w_in", 1, 0, 3),
    ("w_dn", 1, 0, 3), ("t_in", 1, 3, 1), ("t_in", 1, 1, 1), ("w_up", 1, 0, 3), ("w_dn", 1, 0, 1),
    ("t_near", 0, 2, 2), ("w_in", 1, 3, 2), ("w_in", 1, 1, 0), ("t_in", 1, 0, 3),
    ("t_up", 1, 0, 3), ("t_dn", 1, 0, 3), ("prod", 2), ("t_up", 1, 3, 0), ("t_in", 1, 3, 2),
    ("t_in", 1, 1, 2), ("w_up", 1, 3, 0), ("w_dn", 1, 1, 2), ("w_far", 0, 2, 1), ("w_in", 1, 3, 1),
    ("w_in", 1, 1, 3), ("t_in", 1, 2, 1), ("t_in", 1, 3, 3), ("t_in", 1, 1, 3), ("t_dn", 1, 1, 3),
    ("w_dn", 1, 1, 3), ("w_in", 1, 3, 3), ("w_in", 1, 1, 1), ("t_in", 1, 2, 2), ("prod", 3),
    ("t_in", 1, 2, 0), ("t_in", 1, 2, 3), ("prod", 4), ("w_in", 1, 2, 0), ("w_in", 1, 2, 2),
    ("w_in", 1, 2, 1), ("w_in", 1, 2, 3),
]


def kernel(x_ref, w_ref, eocc, evirt, nocc, nvirt, window, out_ref, xbuf, wbuf, tbuf, abuf, s32, lhs,
           inv, acc, w_rs, s_rs, t_rs, a_rs, ss, loc, out_sem):
    row = lax.axis_index("row")
    col = lax.axis_index("col")
    z, xl = row // 2, row % 2
    xh, y, core = col // 8, (col // 2) % 4, col % 2
    sgn = 1 - 2 * core
    g = window[0]

    def col_of(a, b, k):
        return a * 8 + b * 2 + k

    y_up = (row, col_of(xh, (y + 4 + sgn) % 4, core))
    y_dn = (row, col_of(xh, (y + 4 - sgn) % 4, core))
    x_far = (row, col_of(1 - xh, y, core))
    sibling = (row, col_of(xh, y, 1 - core))
    z_up = (((z + 4 + sgn) % 4) * 2 + xl, col)
    z_dn = (((z + 4 - sgn) % 4) * 2 + xl, col)
    x_near = (z * 2 + 1 - xl, col)
    others = [(dx, dy, dk) for dx in range(2) for dy in (0, 1, 3, 2) for dk in range(2)
              if (dx, dy, dk) != (0, 0, 0)]

    def peer(d):
        return col_of((xh + d[0]) % 2, (y + d[1]) % 4, (core + d[2]) % 2)

    barrier = pltpu.get_barrier_semaphore()
    for d in others:
        pl.semaphore_signal(barrier, inc=1, device_id=(row, peer(d)), device_id_type=MESH)
    for dev in (z_up, z_dn, x_near):
        pl.semaphore_signal(barrier, inc=1, device_id=dev, device_id_type=MESH)

    amps = pltpu.make_async_copy(x_ref, xbuf, loc.at[0])
    amps.start()
    mine = pltpu.make_async_copy(w_ref, wbuf.at[xh * 4 + y, core], loc.at[1])
    mine.start()
    amps.wait()

    rid = lax.broadcasted_iota(jnp.int32, (64, 128), 0)
    lane = lax.broadcasted_iota(jnp.int32, (64, 128), 1)
    live_src = (rid % OCC < nocc[row]) & (col * 4 + rid // OCC < nvirt[row ^ g])

    def prepare(h2, _):
        for p in range(OCC):
            s32[pl.ds(p, 64, stride=OCC), 0:VIR] = xbuf[h2, p].astype(jnp.float32)
        for pair in range(8):
            lo = s32[pl.ds(pair * 128, 64), :]
            hi = pltpu.roll(s32[pl.ds(pair * 128 + 64, 64), :], 64, 1)
            both = jnp.where(live_src, jnp.where(lane < VIR, lo, hi), 0.0)
            lhs[pl.ds(h2 * 64, 64), pl.ds(pair * 128, 128)] = both.astype(jnp.bfloat16)
        return 0

    lax.fori_loop(0, NIRREP, prepare, 0)
    mine.wait()
    pl.semaphore_wait(barrier, len(others) + 3)

    sends = []
    waiting = []
    in_flight = {}

    def push(src, dst, rsem, dev, way=None):
        queue = in_flight.setdefault(way, [])
        if way is not None and len(queue) == DEPTH:
            queue.pop(0).wait_send()
        cp = pltpu.make_async_remote_copy(
            src_ref=src, dst_ref=dst, send_sem=ss.at[len(sends)], recv_sem=rsem,
            device_id=dev, device_id_type=MESH)
        cp.start()
        sends.append(cp)
        queue.append(cp)

    def arrived(ref, rsem):
        pltpu.make_async_remote_copy(
            src_ref=ref, dst_ref=ref, send_sem=ss.at[N_SENDS - 1], recv_sem=rsem,
            device_id=sibling, device_id_type=MESH).wait_recv()

    def wslot(da, db, j):
        return wbuf.at[((xh + da) % 2) * 4 + (y + 4 + sgn * db) % 4, core, pl.ds(j * PART, PART)]

    def trows(j):
        return pl.multiple_of(((xh + j // 2) % 2) * 512 + ((y // 2 + j % 2) % 2) * 256, 256)

    def tslot(da, db, j):
        return tbuf.at[((z + 4 + sgn * db) % 4) * 2 + (xl + da) % 2, pl.ds(trows(j), PART)]

    def send(op, da, db, j):
        slot, sems = (wslot, w_rs) if op[0] == "w" else (tslot, t_rs)
        dev, da2, db2 = {
            "w_up": (y_up, da, db + 3), "w_dn": (y_dn, da, db + 1), "w_far": (x_far, 1 - da, db),
            "t_up": (z_up, da, db + 3), "t_dn": (z_dn, da, db + 1), "t_near": (x_near, 1 - da, db),
        }[op]
        ref = slot(da, db, j)
        way = "x" if op in ("w_far", "t_near") else op
        push(ref, ref, sems.at[da2, db2 % 4, j], dev, way)

    def share(da, db, j):
        ref = wslot(da, db, j)
        push(ref, ref, s_rs.at[da, db, j], sibling)
        waiting.append((da, db, j))

    def w_in(da, db, j):
        arrived(wslot(da, db, j), w_rs.at[da, db, j])
        share(da, db, j)

    def t_in(da, db, j):
        if (da, db) != (0, 0):
            arrived(tslot(da, db, j), t_rs.at[da, db, j])
            return
        a = (xh + j // 2) % 2
        for i in range(2):
            for k in range(2):
                b = ((y // 2 + j % 2) % 2) * 2 + (y + i) % 2
                if (j, i, k) != (0, 0, 0):
                    c = col_of(a, b, (core + k) % 2)
                    arrived(piece(c), a_rs.at[c])

    def shared(da, db, j):
        ref = wbuf.at[((xh + da) % 2) * 4 + (y + 4 - sgn * db) % 4, 1 - core, pl.ds(j * PART, PART)]
        arrived(ref, s_rs.at[da, db, j])

    def piece(c):
        return tbuf.at[row, pl.ds(pl.multiple_of(c * 64, 64), 64)]

    for op in FIRST:
        send(*op)
    for j in range(4):
        share(0, 0, j)

    src = lax.broadcasted_iota(jnp.int32, (1024, 256), 0)
    dst = lax.broadcasted_iota(jnp.int32, (1024, 256), 1)
    code = (src % VIR) * OCC + src // VIR
    for n in range(4):
        onehot = jnp.where(code == dst + n * 256, 1.0, 0.0).astype(jnp.bfloat16)
        moved = jnp.dot(lhs[...], onehot, preferred_element_type=jnp.float32).astype(jnp.bfloat16)
        for h2 in range(NIRREP):
            abuf[h2 * 2 + n // 2, :, (n % 2) * 256:(n % 2) * 256 + 256] = moved[h2 * 64:h2 * 64 + 64, :]

    for d in others:
        push(abuf.at[peer(d)], piece(col), a_rs.at[col], (row, peer(d)))
    tbuf[row, pl.ds(pl.multiple_of(col * 64, 64), 64), :] = abuf[col]

    h2 = col // 2
    jj = lax.broadcasted_iota(jnp.int32, (OCC, BLOCK), 1)
    ii = lax.broadcasted_iota(jnp.int32, (OCC, BLOCK), 0)
    c_occ = jnp.zeros((OCC, BLOCK), jnp.float32)
    r_occ = jnp.zeros((OCC, BLOCK), jnp.float32)
    for p in range(OCC):
        c_occ = jnp.where(jj % OCC == p, eocc[h2, p], c_occ)
        r_occ = jnp.where(ii == p, eocc[row, p], r_occ)
    c_vir = jnp.zeros((OCC, BLOCK), jnp.float32)
    for q in range(32):
        c_vir = jnp.where(jj // OCC == q, evirt[h2 ^ g, core * 32 + q], c_vir)
    c_e = c_occ - c_vir
    ok = (jj % OCC < nocc[h2]) & (core * 32 + jj // OCC < nvirt[h2 ^ g]) & (ii < nocc[row])
    n_row = nvirt[row ^ g]

    def factor(q, _):
        e = (r_occ - evirt[row ^ g, q]) + c_e
        inv[pl.ds(pl.multiple_of(q * OCC, OCC), OCC), :] = jnp.where(ok & (q < n_row), 1.0 / e, 0.0)
        return 0

    lax.fori_loop(0, VIR, factor, 0)
    acc[...] = jnp.zeros_like(acc)

    def part(h, rows):
        return (jnp.dot(wbuf[h, 0, rows, :], tbuf[h, 0:512, :], preferred_element_type=jnp.float32)
                + jnp.dot(wbuf[h, 1, rows, :], tbuf[h, 512:1024, :], preferred_element_type=jnp.float32))

    def product(h):
        def step(m, _):
            rows = pl.ds(pl.multiple_of(m * TILE, TILE), TILE)
            acc[rows, :] += part(h, rows)
            return 0
        lax.fori_loop(0, ROWS // TILE, step, 0)

    def rank(da, db):
        dist = (db * (4 - db) + 2) // 3
        return da * (2 + dist) + (1 - da) * (dist // 2)

    def stage_of(da, db):
        d = min(db, 4 - db)
        return 2 + d if da else d // 2

    def products(stage):
        for key in [k for k in waiting if stage_of(*k[:2]) <= stage and stage < 4]:
            waiting.remove(key)
            shared(*key)

        def each(h, _):
            by_w = rank((h // 4 + xh) % 2, (h % 4 + 4 - y) % 4)
            by_t = rank((h % 2 + xl) % 2, (h // 2 + 4 - z) % 4)

            @pl.when((by_w <= stage) & (by_t <= stage) & ((by_w == stage) | (by_t == stage)) & (by_w < 4))
            def _():
                product(h)
            return 0

        lax.fori_loop(0, NIRREP, each, 0)

    for op in ORDER:
        if op in FIRST:
            continue
        if op[0] == "prod":
            products(op[1])
        elif op[0] == "w_in":
            w_in(*op[1:])
        elif op[0] == "t_in":
            t_in(*op[1:])
        else:
            send(*op)

    last = (1 - xh) * 4 + (y + 2) % 4
    copies = []
    for key in waiting:
        shared(*key)
    for m in range(ROWS // PART):
        rows = pl.ds(m * PART, PART)
        acc[rows, :] = (acc[rows, :] + part(last, rows)) * inv[rows, :]
        cp = pltpu.make_async_copy(acc.at[rows], out_ref.at[rows], out_sem.at[m])
        cp.start()
        copies.append(cp)
    for queue in in_flight.values():
        for cp in queue:
            cp.wait_send()
    for cp in copies:
        cp.wait()


def per_device(t2_pairs, cycle_ints, eps_occ, eps_virt, occ_count, virt_count, window_irrep):
    amps = t2_pairs.reshape(NIRREP, OCC, OCC * t2_pairs.shape[4], VIR)
    hbm = pl.BlockSpec(memory_space=pl.ANY)
    smem = pl.BlockSpec(memory_space=pltpu.SMEM)
    return pl.pallas_call(
        kernel,
        out_shape=jax.ShapeDtypeStruct((ROWS, BLOCK), jnp.float32),
        in_specs=[hbm, hbm, smem, smem, smem, smem, smem],
        out_specs=hbm,
        scratch_shapes=[
            pltpu.VMEM((NIRREP, OCC, 64, VIR), jnp.bfloat16),
            pltpu.VMEM((NIRREP, 2, ROWS, BLOCK), jnp.bfloat16),
            pltpu.VMEM((NIRREP, ROWS, BLOCK), jnp.bfloat16),
            pltpu.VMEM((16, 64, BLOCK), jnp.bfloat16),
            pltpu.VMEM((1024, 128), jnp.float32),
            pltpu.VMEM((512, 1024), jnp.bfloat16),
            pltpu.VMEM((ROWS, BLOCK), jnp.float32),
            pltpu.VMEM((ROWS, BLOCK), jnp.float32),
            pltpu.SemaphoreType.DMA((2, 4, 4)),
            pltpu.SemaphoreType.DMA((2, 4, 4)),
            pltpu.SemaphoreType.DMA((2, 4, 4)),
            pltpu.SemaphoreType.DMA((16,)),
            pltpu.SemaphoreType.DMA((N_SENDS,)),
            pltpu.SemaphoreType.DMA((2,)),
            pltpu.SemaphoreType.DMA((ROWS // PART,)),
        ],
        compiler_params=pltpu.CompilerParams(
            collective_id=0, has_side_effects=True, vmem_limit_bytes=63 << 20),
    )(amps, cycle_ints, eps_occ, eps_virt, occ_count, virt_count, window_irrep)


def solution(mesh):
    placed = (P("row", None, None, None, "col", None), P("row", "col"), P(), P(), P(), P(), P())
    return jax.shard_map(
        per_device, mesh=mesh, in_specs=placed, out_specs=P("row", "col"), check_vma=False
    )
```

time: 122 us -> 98.9 us (0.81)
  Pallas kernels: 113 us -> 95 us
  local copies, waits for them, and re-layouts: 6.98 us -> 3.08 us
    pallas_call x1, Pallas kernels: 113 us -> 95 us  [per_device(): pl.pallas_call(kernel, out_shape=jax.ShapeDtypeStruct((ROWS, BLOCK), jnp....]
    unnamed x11 -> x1, local copies, waits for them, and re-layouts: 6.98 us -> 3.08 us
where the time goes in v2:
time: 98.9 us; the launch traced here: 98.8 us
  Pallas kernels  95 us (96%)
  local copies, waits for them, and re-layouts  3.08 us (3%)
    pallas_call x1, Pallas kernels, per_device(): pl.pallas_call(kernel, out_shape=jax.ShapeDtypeStruct((ROWS, BLOCK), jnp....  95 us
    unnamed x1, local copies, waits for them, and re-layouts  3.08 us

profile of v2, /device:TPU:9, one launch (start us, length us, event | category | flops | bytes accessed | tf_op | source)
XLA Modules:
  0.0 98.8 jit_solution(4933646429714342979)
XLA Ops:
  0.7 95.0 %shard_map.73 = f32[1024,512]{1,0:T(8,128)} custom-call(bf16[8,16,64,64]{3,2,1,0:T(8,128)(2,1)} %bitcast.1, bf16[1024,512]{1,0:T(8,128)(2,1)} %w_ref.1, f32[8,16]{1,0:T(8,128)} %eocc.1, f32[8,64]{1,0:T(8,128)} %evirt.1, s32[8]{0:T(128)} %nocc.1, s32[8]{0:T(128)} %nvirt.1, s32[1]{0:T(128)S(6)} %copy.9.window), custom_call_target="tpu_custom_call" | custom-call | tf_op jit(solution)/shard_map/pallas_call | solution.py:280
  95.7 3.1 %copy.10 = f32[1024,512]{1,0:T(8,128)} copy(f32[1024,512]{1,0:T(8,128)} %shard_map.73) | data formatting | bytes 4194304

commit v3 on v2

--- a/solution.py
+++ b/solution.py
@@ -14,35 +14,35 @@
 PART = 256
 TILE = 512
 N_SENDS = 110
-DEPTH = 2
+DEPTH = 3
 FIRST = [("w_up", 0, 0, 0), ("w_dn", 0, 0, 2), ("w_far", 0, 0, 0)]
 ORDER = [
     ("w_up", 0, 0, 0), ("w_dn", 0, 0, 2), ("w_far", 0, 0, 0), ("w_up", 0, 0, 1), ("w_dn", 0, 0, 3),
     ("w_in", 0, 3, 0), ("w_in", 0, 1, 2), ("w_in", 1, 0, 0), ("t_in", 0, 0, 0), ("t_up", 0, 0, 0),
     ("t_dn", 0, 0, 0), ("t_near", 0, 0, 0), ("t_in", 0, 0, 1), ("t_up", 0, 0, 1),
-    ("t_dn", 0, 0, 1), ("t_in", 0, 0, 2), ("t_up", 0, 0, 2), ("t_dn", 0, 0, 2), ("t_in", 0, 3, 0),
-    ("t_in", 0, 1, 0), ("w_up", 0, 0, 2), ("w_dn", 0, 0, 0), ("w_far", 0, 0, 2), ("t_in", 0, 0, 3),
-    ("t_up", 0, 0, 3), ("t_dn", 0, 0, 3), ("t_in", 0, 3, 1), ("t_in", 0, 1, 1), ("w_up", 0, 0, 3),
-    ("w_dn", 0, 0, 1), ("t_near", 0, 0, 1), ("w_in", 0, 3, 1), ("w_in", 0, 1, 3),
-    ("t_in", 1, 0, 0), ("t_up", 0, 3, 0), ("t_in", 0, 3, 2), ("t_in", 0, 1, 2), ("t_dn", 0, 1, 2),
-    ("w_up", 0, 3, 0), ("w_dn", 0, 1, 2), ("w_far", 0, 0, 1), ("w_in", 0, 3, 2), ("w_in", 0, 1, 0),
-    ("w_in", 1, 0, 2), ("t_up", 0, 3, 1), ("t_in", 0, 3, 3), ("t_in", 0, 1, 3), ("t_dn", 0, 1, 3),
-    ("w_up", 0, 3, 1), ("w_dn", 0, 1, 3), ("t_near", 0, 0, 2), ("w_in", 0, 3, 3),
-    ("w_in", 0, 1, 1), ("t_in", 1, 0, 1), ("prod", 0), ("t_up", 1, 0, 0), ("t_dn", 1, 0, 0),
-    ("t_in", 0, 2, 0), ("t_in", 0, 2, 2), ("w_up", 1, 0, 0), ("w_dn", 1, 0, 2), ("w_far", 0, 0, 3),
-    ("w_in", 0, 2, 0), ("w_in", 0, 2, 2), ("w_in", 1, 0, 1), ("t_up", 1, 0, 1), ("t_dn", 1, 0, 1),
-    ("t_in", 0, 2, 1), ("t_in", 0, 2, 3), ("w_up", 1, 0, 2), ("w_dn", 1, 0, 0),
-    ("t_near", 0, 0, 3), ("w_in", 0, 2, 1), ("w_in", 0, 2, 3), ("t_in", 1, 0, 2), ("prod", 1),
-    ("t_up", 1, 0, 2), ("t_dn", 1, 0, 2), ("t_in", 1, 3, 0), ("t_in", 1, 1, 0), ("w_up", 1, 0, 1),
-    ("t_near", 0, 2, 1), ("w_in", 1, 3, 0), ("w_in", 1, 1, 2), ("w_in", 1, 0, 3),
-    ("w_dn", 1, 0, 3), ("t_in", 1, 3, 1), ("t_in", 1, 1, 1), ("w_up", 1, 0, 3), ("w_dn", 1, 0, 1),
-    ("t_near", 0, 2, 2), ("w_in", 1, 3, 2), ("w_in", 1, 1, 0), ("t_in", 1, 0, 3),
-    ("t_up", 1, 0, 3), ("t_dn", 1, 0, 3), ("prod", 2), ("t_up", 1, 3, 0), ("t_in", 1, 3, 2),
-    ("t_in", 1, 1, 2), ("w_up", 1, 3, 0), ("w_dn", 1, 1, 2), ("w_far", 0, 2, 1), ("w_in", 1, 3, 1),
-    ("w_in", 1, 1, 3), ("t_in", 1, 2, 1), ("t_in", 1, 3, 3), ("t_in", 1, 1, 3), ("t_dn", 1, 1, 3),
-    ("w_dn", 1, 1, 3), ("w_in", 1, 3, 3), ("w_in", 1, 1, 1), ("t_in", 1, 2, 2), ("prod", 3),
-    ("t_in", 1, 2, 0), ("t_in", 1, 2, 3), ("prod", 4), ("w_in", 1, 2, 0), ("w_in", 1, 2, 2),
-    ("w_in", 1, 2, 1), ("w_in", 1, 2, 3),
+    ("t_dn", 0, 0, 1), ("w_up", 0, 0, 2), ("w_dn", 0, 0, 0), ("w_far", 0, 0, 2), ("t_in", 0, 0, 2),
+    ("t_up", 0, 0, 2), ("t_dn", 0, 0, 2), ("t_in", 0, 3, 0), ("t_in", 0, 1, 0), ("t_in", 0, 0, 3),
+    ("t_up", 0, 0, 3), ("t_dn", 0, 0, 3), ("w_up", 0, 0, 3), ("w_dn", 0, 0, 1),
+    ("t_near", 0, 0, 1), ("t_in", 0, 3, 1), ("t_in", 0, 1, 1), ("w_in", 0, 3, 1),
+    ("w_in", 0, 1, 3), ("t_in", 1, 0, 0), ("t_up", 0, 3, 0), ("w_up", 0, 3, 0), ("w_dn", 0, 1, 2),
+    ("w_far", 0, 0, 1), ("t_in", 0, 3, 2), ("t_in", 0, 1, 2), ("t_dn", 0, 1, 2), ("w_in", 0, 3, 2),
+    ("w_in", 0, 1, 0), ("w_in", 1, 0, 2), ("t_up", 0, 3, 1), ("w_up", 0, 3, 1), ("w_dn", 0, 1, 3),
+    ("t_near", 0, 0, 2), ("t_in", 0, 3, 3), ("t_in", 0, 1, 3), ("t_dn", 0, 1, 3),
+    ("w_in", 0, 3, 3), ("w_in", 0, 1, 1), ("t_in", 1, 0, 1), ("t_up", 1, 0, 0), ("t_dn", 1, 0, 0),
+    ("w_up", 1, 0, 0), ("w_dn", 1, 0, 2), ("w_far", 0, 0, 3), ("prod", 0, 0), ("t_in", 0, 2, 0),
+    ("t_in", 0, 2, 2), ("w_in", 0, 2, 0), ("w_in", 0, 2, 2), ("w_in", 1, 0, 1), ("prod", 0, 1),
+    ("t_up", 1, 0, 1), ("t_dn", 1, 0, 1), ("w_up", 1, 0, 2), ("w_dn", 1, 0, 0),
+    ("t_near", 0, 0, 3), ("t_in", 0, 2, 1), ("t_in", 0, 2, 3), ("w_in", 0, 2, 1),
+    ("w_in", 0, 2, 3), ("t_in", 1, 0, 2), ("t_up", 1, 0, 2), ("t_dn", 1, 0, 2), ("w_up", 1, 0, 1),
+    ("t_near", 0, 2, 1), ("prod", 1, 0), ("t_in", 1, 3, 0), ("t_in", 1, 1, 0), ("w_in", 1, 3, 0),
+    ("w_in", 1, 1, 2), ("w_in", 1, 0, 3), ("w_dn", 1, 0, 3), ("prod", 1, 1), ("w_up", 1, 0, 3),
+    ("w_dn", 1, 0, 1), ("w_far", 0, 2, 1), ("t_in", 1, 3, 1), ("t_in", 1, 1, 1), ("w_in", 1, 3, 2),
+    ("w_in", 1, 1, 0), ("t_in", 1, 0, 3), ("t_up", 1, 0, 3), ("t_dn", 1, 0, 3), ("t_up", 1, 3, 0),
+    ("w_up", 1, 3, 0), ("w_far", 0, 2, 2), ("prod", 2, 0), ("t_in", 1, 3, 2), ("t_in", 1, 1, 2),
+    ("t_dn", 1, 1, 2), ("w_in", 1, 3, 1), ("w_in", 1, 1, 3), ("t_in", 1, 2, 1), ("w_dn", 1, 1, 3),
+    ("prod", 2, 1), ("t_in", 1, 3, 3), ("t_in", 1, 1, 3), ("t_dn", 1, 1, 3), ("w_in", 1, 3, 3),
+    ("w_in", 1, 1, 1), ("w_in", 1, 2, 1), ("prod", 3, 0), ("t_in", 1, 2, 0), ("t_in", 1, 2, 2),
+    ("w_in", 1, 2, 0), ("w_in", 1, 2, 3), ("w_in", 1, 2, 2), ("prod", 3, 1), ("t_in", 1, 2, 3),
 ]
 
 
@@ -81,25 +81,6 @@
     amps.start()
     mine = pltpu.make_async_copy(w_ref, wbuf.at[xh * 4 + y, core], loc.at[1])
     mine.start()
-    amps.wait()
-
-    rid = lax.broadcasted_iota(jnp.int32, (64, 128), 0)
-    lane = lax.broadcasted_iota(jnp.int32, (64, 128), 1)
-    live_src = (rid % OCC < nocc[row]) & (col * 4 + rid // OCC < nvirt[row ^ g])
-
-    def prepare(h2, _):
-        for p in range(OCC):
-            s32[pl.ds(p, 64, stride=OCC), 0:VIR] = xbuf[h2, p].astype(jnp.float32)
-        for pair in range(8):
-            lo = s32[pl.ds(pair * 128, 64), :]
-            hi = pltpu.roll(s32[pl.ds(pair * 128 + 64, 64), :], 64, 1)
-            both = jnp.where(live_src, jnp.where(lane < VIR, lo, hi), 0.0)
-            lhs[pl.ds(h2 * 64, 64), pl.ds(pair * 128, 128)] = both.astype(jnp.bfloat16)
-        return 0
-
-    lax.fori_loop(0, NIRREP, prepare, 0)
-    mine.wait()
-    pl.semaphore_wait(barrier, len(others) + 3)
 
     sends = []
     waiting = []
@@ -168,6 +149,25 @@
     def piece(c):
         return tbuf.at[row, pl.ds(pl.multiple_of(c * 64, 64), 64)]
 
+    amps.wait()
+
+    rid = lax.broadcasted_iota(jnp.int32, (64, 128), 0)
+    lane = lax.broadcasted_iota(jnp.int32, (64, 128), 1)
+    live_src = (rid % OCC < nocc[row]) & (col * 4 + rid // OCC < nvirt[row ^ g])
+
+    def prepare(h2, _):
+        for p in range(OCC):
+            s32[pl.ds(p, 64, stride=OCC), 0:VIR] = xbuf[h2, p].astype(jnp.float32)
+        for pair in range(8):
+            lo = s32[pl.ds(pair * 128, 64), :]
+            hi = pltpu.roll(s32[pl.ds(pair * 128 + 64, 64), :], 64, 1)
+            both = jnp.where(live_src, jnp.where(lane < VIR, lo, hi), 0.0)
+            lhs[pl.ds(h2 * 64, 64), pl.ds(pair * 128, 128)] = both.astype(jnp.bfloat16)
+        return 0
+
+    lax.fori_loop(0, NIRREP, prepare, 0)
+    mine.wait()
+    pl.semaphore_wait(barrier, len(others) + 3)
     for op in FIRST:
         send(*op)
     for j in range(4):
@@ -213,12 +213,9 @@
         return (jnp.dot(wbuf[h, 0, rows, :], tbuf[h, 0:512, :], preferred_element_type=jnp.float32)
                 + jnp.dot(wbuf[h, 1, rows, :], tbuf[h, 512:1024, :], preferred_element_type=jnp.float32))
 
-    def product(h):
-        def step(m, _):
-            rows = pl.ds(pl.multiple_of(m * TILE, TILE), TILE)
-            acc[rows, :] += part(h, rows)
-            return 0
-        lax.fori_loop(0, ROWS // TILE, step, 0)
+    def product(h, m):
+        rows = pl.ds(m * TILE, TILE)
+        acc[rows, :] += part(h, rows)
 
     def rank(da, db):
         dist = (db * (4 - db) + 2) // 3
@@ -228,8 +225,11 @@
         d = min(db, 4 - db)
         return 2 + d if da else d // 2
 
-    def products(stage):
-        for key in [k for k in waiting if stage_of(*k[:2]) <= stage and stage < 4]:
+    last_w = (1 - xh) * 4 + (y + 2) % 4
+    last_t = ((z + 2) % 4) * 2 + 1 - xl
+
+    def products(stage, m):
+        for key in [k for k in waiting if stage_of(*k[:2]) <= stage]:
             waiting.remove(key)
             shared(*key)
 
@@ -237,35 +237,51 @@
             by_w = rank((h // 4 + xh) % 2, (h % 4 + 4 - y) % 4)
             by_t = rank((h % 2 + xl) % 2, (h // 2 + 4 - z) % 4)
 
-            @pl.when((by_w <= stage) & (by_t <= stage) & ((by_w == stage) | (by_t == stage)) & (by_w < 4))
+            @pl.when((by_w <= stage) & (by_t <= stage) & ((by_w == stage) | (by_t == stage)))
             def _():
-                product(h)
+                product(h, m)
             return 0
 
         lax.fori_loop(0, NIRREP, each, 0)
 
+    def quarter(j):
+
+        @pl.when(last_w != last_t)
+        def _():
+            cols = pl.ds(pl.multiple_of(((y // 2 + j % 2) % 2) * 256, 256), 256)
+            for m in range(ROWS // TILE):
+                rows = pl.ds(m * TILE, TILE)
+                acc[rows, :] += jnp.dot(wbuf[last_t, (xh + j // 2) % 2, rows, cols],
+                                        tbuf[last_t, pl.ds(trows(j), PART), :],
+                                        preferred_element_type=jnp.float32)
+
+    copies = []
+
+    def finish(da, db, j):
+        waiting.remove((da, db, j))
+        shared(da, db, j)
+        rows = pl.ds(j * PART, PART)
+        acc[rows, :] = (acc[rows, :] + part(last_w, rows)) * inv[rows, :]
+        cp = pltpu.make_async_copy(acc.at[rows], out_ref.at[rows], out_sem.at[j])
+        cp.start()
+        copies.append(cp)
+
+    final = [op for op in ORDER if op[0] == "w_in" and op[1:3] == (1, 2)]
     for op in ORDER:
         if op in FIRST:
             continue
         if op[0] == "prod":
-            products(op[1])
+            products(*op[1:])
         elif op[0] == "w_in":
             w_in(*op[1:])
         elif op[0] == "t_in":
             t_in(*op[1:])
         else:
             send(*op)
-
-    last = (1 - xh) * 4 + (y + 2) % 4
-    copies = []
-    for key in waiting:
-        shared(*key)
-    for m in range(ROWS // PART):
-        rows = pl.ds(m * PART, PART)
-        acc[rows, :] = (acc[rows, :] + part(last, rows)) * inv[rows, :]
-        cp = pltpu.make_async_copy(acc.at[rows], out_ref.at[rows], out_sem.at[m])
-        cp.start()
-        copies.append(cp)
+    for j in range(4):
+        quarter(j)
+    for i, op in enumerate(final):
+        finish(*op[1:])
     for queue in in_flight.values():
         for cp in queue:
             cp.wait_send()

time: 98.9 us -> 97.4 us (0.985); the launches traced: 98.8 us -> 96.2 us
  Pallas kernels: 95 us -> 92.4 us
    pallas_call x1, Pallas kernels: 95 us -> 92.4 us  [per_device(): pl.pallas_call(kernel, out_shape=jax.ShapeDtypeStruct((ROWS, BLOCK), jnp....]
where the time goes in v3:
time: 97.4 us; the launch traced here: 96.2 us
  Pallas kernels  92.4 us (95%)
  local copies, waits for them, and re-layouts  3.08 us (3%)
    pallas_call x1, Pallas kernels, per_device(): pl.pallas_call(kernel, out_shape=jax.ShapeDtypeStruct((ROWS, BLOCK), jnp....  92.4 us
    unnamed x1, local copies, waits for them, and re-layouts  3.08 us

profile of v3, /device:TPU:9, one launch (start us, length us, event | category | flops | bytes accessed | tf_op | source)
XLA Modules:
  0.0 96.2 jit_solution(14980449388051301706)
XLA Ops:
  0.7 92.4 %shard_map.73 = f32[1024,512]{1,0:T(8,128)} custom-call(bf16[8,16,64,64]{3,2,1,0:T(8,128)(2,1)} %bitcast.1, bf16[1024,512]{1,0:T(8,128)(2,1)} %w_ref.1, f32[8,16]{1,0:T(8,128)} %eocc.1, f32[8,64]{1,0:T(8,128)} %evirt.1, s32[8]{0:T(128)} %nocc.1, s32[8]{0:T(128)} %nvirt.1, s32[1]{0:T(128)S(6)} %copy.9.window), custom_call_target="tpu_custom_call" | custom-call | tf_op jit(solution)/shard_map/pallas_call | solution.py:296
  93.1 3.1 %copy.10 = f32[1024,512]{1,0:T(8,128)} copy(f32[1024,512]{1,0:T(8,128)} %shard_map.73) | data formatting | bytes 4194304

commit v4 on v3

--- a/solution.py
+++ b/solution.py
@@ -46,8 +46,8 @@
 ]
 
 
-def kernel(x_ref, w_ref, eocc, evirt, nocc, nvirt, window, out_ref, xbuf, wbuf, tbuf, abuf, s32, lhs,
-           inv, acc, w_rs, s_rs, t_rs, a_rs, ss, loc, out_sem):
+def kernel(x_ref, w_ref, eocc, evirt, nocc, nvirt, window, acc, xbuf, wbuf, tbuf, abuf, s32, lhs,
+           inv, w_rs, s_rs, t_rs, a_rs, ss, loc):
     row = lax.axis_index("row")
     col = lax.axis_index("col")
     z, xl = row // 2, row % 2
@@ -255,16 +255,11 @@
                                         tbuf[last_t, pl.ds(trows(j), PART), :],
                                         preferred_element_type=jnp.float32)
 
-    copies = []
-
     def finish(da, db, j):
         waiting.remove((da, db, j))
         shared(da, db, j)
         rows = pl.ds(j * PART, PART)
         acc[rows, :] = (acc[rows, :] + part(last_w, rows)) * inv[rows, :]
-        cp = pltpu.make_async_copy(acc.at[rows], out_ref.at[rows], out_sem.at[j])
-        cp.start()
-        copies.append(cp)
 
     final = [op for op in ORDER if op[0] == "w_in" and op[1:3] == (1, 2)]
     for op in ORDER:
@@ -285,19 +280,18 @@
     for queue in in_flight.values():
         for cp in queue:
             cp.wait_send()
-    for cp in copies:
-        cp.wait()
 
 
 def per_device(t2_pairs, cycle_ints, eps_occ, eps_virt, occ_count, virt_count, window_irrep):
     amps = t2_pairs.reshape(NIRREP, OCC, OCC * t2_pairs.shape[4], VIR)
     hbm = pl.BlockSpec(memory_space=pl.ANY)
+    vmem = pl.BlockSpec(memory_space=pltpu.VMEM)
     smem = pl.BlockSpec(memory_space=pltpu.SMEM)
     return pl.pallas_call(
         kernel,
-        out_shape=jax.ShapeDtypeStruct((ROWS, BLOCK), jnp.float32),
+        out_shape=pltpu.VMEM((ROWS, BLOCK), jnp.float32),
         in_specs=[hbm, hbm, smem, smem, smem, smem, smem],
-        out_specs=hbm,
+        out_specs=vmem,
         scratch_shapes=[
             pltpu.VMEM((NIRREP, OCC, 64, VIR), jnp.bfloat16),
             pltpu.VMEM((NIRREP, 2, ROWS, BLOCK), jnp.bfloat16),
@@ -306,17 +300,15 @@
             pltpu.VMEM((1024, 128), jnp.float32),
             pltpu.VMEM((512, 1024), jnp.bfloat16),
             pltpu.VMEM((ROWS, BLOCK), jnp.float32),
-            pltpu.VMEM((ROWS, BLOCK), jnp.float32),
             pltpu.SemaphoreType.DMA((2, 4, 4)),
             pltpu.SemaphoreType.DMA((2, 4, 4)),
             pltpu.SemaphoreType.DMA((2, 4, 4)),
             pltpu.SemaphoreType.DMA((16,)),
             pltpu.SemaphoreType.DMA((N_SENDS,)),
             pltpu.SemaphoreType.DMA((2,)),
-            pltpu.SemaphoreType.DMA((ROWS // PART,)),
         ],
         compiler_params=pltpu.CompilerParams(
-            collective_id=0, has_side_effects=True, vmem_limit_bytes=63 << 20),
+            collective_id=0, has_side_effects=True, vmem_limit_bytes=58 << 20),
     )(amps, cycle_ints, eps_occ, eps_virt, occ_count, virt_count, window_irrep)
 
 

time: 97.4 us -> 94.9 us (0.974)
  local copies, waits for them, and re-layouts: 3.08 us -> 1.32 us
    unnamed x1, local copies, waits for them, and re-layouts: 3.08 us -> 1.32 us
where the time goes in v4:
time: 94.9 us; the launch traced here: 93.7 us
  Pallas kernels  91.7 us (97%)
  local copies, waits for them, and re-layouts  1.32 us (1%)
    pallas_call x1, Pallas kernels, per_device(): pl.pallas_call(kernel, out_shape=pltpu.VMEM((ROWS, BLOCK), jnp.float32),...  91.7 us

profile of v4, /device:TPU:9, one launch (start us, length us, event | category | flops | bytes accessed | tf_op | source)
XLA Modules:
  0.0 93.7 jit_solution(846194085330892217)
XLA Ops:
  0.7 91.7 %shard_map.73 = f32[1024,512]{1,0:T(8,128)S(1)} custom-call(bf16[8,16,64,64]{3,2,1,0:T(8,128)(2,1)} %bitcast.1, bf16[1024,512]{1,0:T(8,128)(2,1)} %w_ref.1, f32[8,16]{1,0:T(8,128)} %eocc.1, f32[8,64]{1,0:T(8,128)} %evirt.1, s32[8]{0:T(128)} %nocc.1, s32[8]{0:T(128)} %nvirt.1, s32[1]{0:T(128)S(6)} %copy.10.window), custom_call_target="tpu_custom_call" | custom-call | tf_op jit(solution)/shard_map/pallas_call | solution.py:290
  92.3 1.3 %copy.9 = f32[1024,512]{1,0:T(8,128)} copy(f32[1024,512]{1,0:T(8,128)S(1)} %shard_map.73) | data formatting | bytes 4194304

commit v5 on v4

--- a/solution.py
+++ b/solution.py
@@ -46,8 +46,8 @@
 ]
 
 
-def kernel(x_ref, w_ref, eocc, evirt, nocc, nvirt, window, acc, xbuf, wbuf, tbuf, abuf, s32, lhs,
-           inv, w_rs, s_rs, t_rs, a_rs, ss, loc):
+def kernel(x_ref, w_ref, eocc, evirt, nocc, nvirt, window, acc, inv, w_last, t_last, xbuf, wbuf, tbuf, abuf, s32, lhs,
+           w_rs, s_rs, t_rs, a_rs, ss, loc):
     row = lax.axis_index("row")
     col = lax.axis_index("col")
     z, xl = row // 2, row % 2
@@ -103,6 +103,8 @@
             device_id=sibling, device_id_type=MESH).wait_recv()
 
     def wslot(da, db, j):
+        if (da, db) == (1, 2):
+            return w_last.at[core, pl.ds(j * PART, PART)]
         return wbuf.at[((xh + da) % 2) * 4 + (y + 4 + sgn * db) % 4, core, pl.ds(j * PART, PART)]
 
     def trows(j):
@@ -118,8 +120,11 @@
             "t_up": (z_up, da, db + 3), "t_dn": (z_dn, da, db + 1), "t_near": (x_near, 1 - da, db),
         }[op]
         ref = slot(da, db, j)
+        there = ref
+        if slot is wslot and (da2, db2 % 4) == (1, 2):
+            there = w_last.at[core, pl.ds(j * PART, PART)]
         way = "x" if op in ("w_far", "t_near") else op
-        push(ref, ref, sems.at[da2, db2 % 4, j], dev, way)
+        push(ref, there, sems.at[da2, db2 % 4, j], dev, way)
 
     def share(da, db, j):
         ref = wslot(da, db, j)
@@ -143,7 +148,7 @@
                     arrived(piece(c), a_rs.at[c])
 
     def shared(da, db, j):
-        ref = wbuf.at[((xh + da) % 2) * 4 + (y + 4 - sgn * db) % 4, 1 - core, pl.ds(j * PART, PART)]
+        ref = w_last.at[1 - core, pl.ds(j * PART, PART)] if (da, db) == (1, 2) else wbuf.at[((xh + da) % 2) * 4 + (y + 4 - sgn * db) % 4, 1 - core, pl.ds(j * PART, PART)]
         arrived(ref, s_rs.at[da, db, j])
 
     def piece(c):
@@ -255,12 +260,6 @@
                                         tbuf[last_t, pl.ds(trows(j), PART), :],
                                         preferred_element_type=jnp.float32)
 
-    def finish(da, db, j):
-        waiting.remove((da, db, j))
-        shared(da, db, j)
-        rows = pl.ds(j * PART, PART)
-        acc[rows, :] = (acc[rows, :] + part(last_w, rows)) * inv[rows, :]
-
     final = [op for op in ORDER if op[0] == "w_in" and op[1:3] == (1, 2)]
     for op in ORDER:
         if op in FIRST:
@@ -273,13 +272,30 @@
             t_in(*op[1:])
         else:
             send(*op)
+    keep = pltpu.make_async_copy(tbuf.at[last_w], t_last, loc.at[0])
+    keep.start()
     for j in range(4):
         quarter(j)
-    for i, op in enumerate(final):
-        finish(*op[1:])
+    for op in final:
+        shared(*op[1:])
+    keep.wait()
     for queue in in_flight.values():
         for cp in queue:
             cp.wait_send()
+
+
+def deliver(acc, inv, w_last, t_last, out_ref, done, sems):
+    copies = []
+    for i in range(ROWS // PART):
+        rows = pl.ds(i * PART, PART)
+        total = jnp.dot(w_last[0, rows, :], t_last[0:512, :], preferred_element_type=jnp.float32)
+        total += jnp.dot(w_last[1, rows, :], t_last[512:1024, :], preferred_element_type=jnp.float32)
+        done[rows, :] = (acc[rows, :] + total) * inv[rows, :]
+        cp = pltpu.make_async_copy(done.at[rows], out_ref.at[rows], sems.at[i])
+        cp.start()
+        copies.append(cp)
+    for cp in copies:
+        cp.wait()
 
 
 def per_device(t2_pairs, cycle_ints, eps_occ, eps_virt, occ_count, virt_count, window_irrep):
@@ -287,11 +303,12 @@
     hbm = pl.BlockSpec(memory_space=pl.ANY)
     vmem = pl.BlockSpec(memory_space=pltpu.VMEM)
     smem = pl.BlockSpec(memory_space=pltpu.SMEM)
-    return pl.pallas_call(
+    parts = pl.pallas_call(
         kernel,
-        out_shape=pltpu.VMEM((ROWS, BLOCK), jnp.float32),
+        out_shape=[pltpu.VMEM((ROWS, BLOCK), jnp.float32)] * 2 + [
+            pltpu.VMEM((2, ROWS, BLOCK), jnp.bfloat16), pltpu.VMEM((ROWS, BLOCK), jnp.bfloat16)],
         in_specs=[hbm, hbm, smem, smem, smem, smem, smem],
-        out_specs=vmem,
+        out_specs=[vmem] * 4,
         scratch_shapes=[
             pltpu.VMEM((NIRREP, OCC, 64, VIR), jnp.bfloat16),
             pltpu.VMEM((NIRREP, 2, ROWS, BLOCK), jnp.bfloat16),
@@ -299,7 +316,6 @@
             pltpu.VMEM((16, 64, BLOCK), jnp.bfloat16),
             pltpu.VMEM((1024, 128), jnp.float32),
             pltpu.VMEM((512, 1024), jnp.bfloat16),
-            pltpu.VMEM((ROWS, BLOCK), jnp.float32),
             pltpu.SemaphoreType.DMA((2, 4, 4)),
             pltpu.SemaphoreType.DMA((2, 4, 4)),
             pltpu.SemaphoreType.DMA((2, 4, 4)),
@@ -308,8 +324,19 @@
             pltpu.SemaphoreType.DMA((2,)),
         ],
         compiler_params=pltpu.CompilerParams(
-            collective_id=0, has_side_effects=True, vmem_limit_bytes=58 << 20),
+            collective_id=0, has_side_effects=True, vmem_limit_bytes=48 << 20),
     )(amps, cycle_ints, eps_occ, eps_virt, occ_count, virt_count, window_irrep)
+    return pl.pallas_call(
+        deliver,
+        out_shape=jax.ShapeDtypeStruct((ROWS, BLOCK), jnp.float32),
+        in_specs=[vmem] * 4,
+        out_specs=hbm,
+        scratch_shapes=[
+            pltpu.VMEM((ROWS, BLOCK), jnp.float32),
+            pltpu.SemaphoreType.DMA((ROWS // PART,)),
+        ],
+        compiler_params=pltpu.CompilerParams(vmem_limit_bytes=6 << 20),
+    )(*parts)
 
 
 def solution(mesh):

time: 94.9 us -> 94 us (level)
  local copies, waits for them, and re-layouts: 1.32 us -> 0 us
    unnamed x1 -> x0, local copies, waits for them, and re-layouts: 1.32 us -> none
    pallas_call x1 -> x2, Pallas kernels: 91.7 us -> 92.1 us  [the longest x1 90 us: per_device(): pl.pallas_call(kernel, out_shape=[pltpu.VMEM((ROWS, BLOCK), jnp.float32)]...]
where the time goes in v5:
time: 94 us; the launch traced here: 92.8 us
  Pallas kernels  92.1 us (98%)
    pallas_call x1, Pallas kernels, per_device(): pl.pallas_call(kernel, out_shape=[pltpu.VMEM((ROWS, BLOCK), jnp.float32)]...  90 us
    pallas_call x1, Pallas kernels, per_device(): pl.pallas_call(deliver, out_shape=jax.ShapeDtypeStruct((ROWS, BLOCK), jnp...  2.09 us

profile of v5, /device:TPU:9, one launch (start us, length us, event | category | flops | bytes accessed | tf_op | source)
XLA Modules:
  0.0 92.8 jit_solution(15164204877953223263)
XLA Ops:
  0.7 90.0 %shard_map.73 = (f32[1024,512]{1,0:T(8,128)S(1)}, f32[1024,512]{1,0:T(8,128)S(1)}, bf16[2,1024,512]{2,1,0:T(8,128)(2,1)S(1)}, bf16[1024,512]{1,0:T(8,128)(2,1)S(1)}) custom-call(bf16[8,16,64,64]{3,2,1,0:T(8,128)(2,1)} %bitcast.1, bf16[1024,512]{1,0:T(8,128)(2,1)} %w_ref.1, f32[8,16]{1,0:T(8,128)} %eocc.1, f32[8,64]{1,0:T(8,128)} %evirt.1, s32[8]{0:T(128)} %nocc.1, ...), custom_call_target="tpu_custom_call" | custom-call | tf_op jit(solution)/shard_map/pallas_call | solution.py:306
  90.7 2.1 %shard_map.74 = f32[1024,512]{1,0:T(8,128)} custom-call(f32[1024,512]{1,0:T(8,128)S(1)} %get-tuple-element.9.acc, f32[1024,512]{1,0:T(8,128)S(1)} %get-tuple-element.10.inv, bf16[2,1024,512]{2,1,0:T(8,128)(2,1)S(1)} %get-tuple-element.11.w_last, bf16[1024,512]{1,0:T(8,128)(2,1)S(1)} %get-tuple-element.12.t_last), custom_call_target="tpu_custom_call" | custom-call | tf_op jit(solution)/shard_map/pallas_call | solution.py:329
